TPU v7x, 32 devices: a whole 2x2x4 slice. The times are simulated.
32 devices in a mesh: tok: 4 (over y, core), ch: 8 (over z, x).
Axes of the slice: x: 2, y: 2, z: 4, core: 2. Of those that a mesh axis runs over, the one named last changes fastest.
Arguments:
- tokens: bfloat16 [4096, 4096], P('tok', 'ch'), may hold values from -6 to 6
- w_in: bfloat16 [4096, 16384], P('tok', 'ch'), may hold values from -0.09375 to 0.09375
- b_in: float32 [16384], P('ch'), may hold values from -3 to 3
- dw_kernel: float32 [9, 16384], P(None, 'ch'), may hold values from -2 to 2
- dw_bias: float32 [16384], P('ch'), may hold values from -3 to 3
- w_out: bfloat16 [16384, 4096], P('ch', 'tok'), may hold values from -0.0625 to 0.0625
- b_out: float32 [4096], P('ch'), may hold values from -3 to 3
Outputs:
- mixed: bfloat16 [4096, 4096], P('tok', 'ch')
All inputs are finite; a program needn't handle non-finite values.
Results may differ from a plain program's by a relative error of at most 0.0055.
Values may be sent and summed in bfloat16 or wider, within the bound.
No kernel may reach another device: no remote copies, remote signals or barrier semaphores. Data moves between devices by JAX's collectives and lax.ppermute only.
A program may use at most 128 MiB of HBM per device.

v0:
```python
import jax
import jax.numpy as jnp
from jax import lax
from jax.sharding import PartitionSpec as P

IMAGES = 2
GRIDW = 64


def with_halo(array, sides, width):
    for axis, dim in sides:
        size, length = (lax.axis_size(axis), array.shape[dim])
        up = [(i, (i + 1) % size) for i in range(size - 1)]
        down = [(j, i) for i, j in up]
        last = lax.slice_in_dim(array, length - width, length, axis=dim)
        initial = lax.slice_in_dim(array, 0, width, axis=dim)
        before = lax.ppermute(last, axis, up)
        after = lax.ppermute(initial, axis, down)
        array = jnp.concatenate([before, array, after], axis=dim)
    return array


def fetch_rims(grid):
    return with_halo(grid, (("tok", 0),), 1)


def conv_taps(padded, taps, bias, height, width):
    conv = bias + jnp.zeros(
        (height,) + padded.shape[1:2] + (width,) + padded.shape[3:], jnp.float32
    )
    for row_off in range(3):
        for col_off in range(3):
            conv = (
                conv
                + taps[3 * row_off + col_off]
                * padded[row_off : row_off + height, :, col_off : col_off + width, :]
            )
    return conv


def pad_columns(grid):
    return jnp.pad(grid, ((0, 0), (0, 0), (1, 1), (0, 0)))


def local(tokens, w_in, b_in, dw_kernel, dw_bias, w_out, b_out):
    rows = tokens.shape[0]
    hidden = w_in.shape[1]
    w_whole = lax.all_gather(w_in, "tok", axis=0, tiled=True)
    summed = jnp.dot(
        lax.all_gather(tokens, "ch", axis=1, tiled=True),
        w_whole,
        preferred_element_type=jnp.float32,
    )
    pre = (summed + b_in).astype(jnp.bfloat16)
    height = rows // (IMAGES * GRIDW)
    grid = pre.reshape(height, IMAGES, GRIDW, hidden)
    padded = pad_columns(fetch_rims(grid).astype(jnp.float32))
    conv = conv_taps(padded, dw_kernel, dw_bias, height, GRIDW)
    act = jax.nn.gelu(conv, approximate=False).astype(jnp.bfloat16).reshape(rows, hidden)
    w_cols = lax.all_gather(w_out, "tok", axis=1, tiled=True)
    flipped = lax.psum_scatter(
        lax.dot_general(w_cols, act, (((0,), (1,)), ((), ())), preferred_element_type=jnp.float32),
        "ch",
        scatter_dimension=0,
        tiled=True,
    )
    return (flipped.T + b_out).astype(jnp.bfloat16)


def solution(mesh):
    in_specs = (
        P("tok", "ch"),
        P("tok", "ch"),
        P("ch"),
        P(None, "ch"),
        P("ch"),
        P("ch", "tok"),
        P("ch"),
    )
    out_specs = P("tok", "ch")
    return jax.shard_map(local, mesh=mesh, in_specs=in_specs, out_specs=out_specs, check_vma=False)
```

profile of v0, /device:TPU:0, one launch (start us, length us, event | category | flops | bytes accessed | tf_op | source)
XLA Modules:
  0.0 669.0 jit_solution(11230460719229125539)
XLA Ops:
  6.5 0.0 copy-start.3
  6.5 0.0 all-gather.4.cloned.1.call-start
  6.5 0.7 all-gather.4.cloned.1.call-update
  7.3 0.0 all-gather.6.cloned.1.call-start
  7.3 0.7 all-gather.6.cloned.1.call-update
  8.0 0.0 all-gather.8.cloned.1.call-start
  8.1 0.7 all-gather.8.cloned.1.call-update
  8.7 0.0 copy-start
  8.8 0.0 reduce-scatter.2.cloned.1.call-start
  8.8 128.3 %all-gather.4.cloned.1.call-done = bf16[1024,4096]{1,0:T(8,128)(2,1)} async-done(((bf16[1024,512]{1,0:T(8,128)(2,1)}), bf16[1024,4096]{1,0:T(8,128)(2,1)}) %all-gather.4.cloned.1.call-update) | async-done | bytes 8388624 | tf_op jit(solution)/shard_map/all_gather | solution.py:50
  137.1 105.7 %all-gather.6.cloned.1.call-done = bf16[4096,2048]{1,0:T(8,128)(2,1)} async-done(((bf16[1024,2048]{1,0:T(8,128)(2,1)}), bf16[4096,2048]{1,0:T(8,128)(2,1)}) %all-gather.6.cloned.1.call-update) | async-done | bytes 16777232 | tf_op jit(solution)/shard_map/all_gather | solution.py:48
  242.7 0.0 copy-done.3
  242.7 22.7 %add_convert_fusion = bf16[1024,2048]{1,0:T(8,128)(2,1)S(1)} fusion(bf16[1024,4096]{1,0:T(8,128)(2,1)} %all-gather.4.cloned.1.call-done, bf16[4096,2048]{1,0:T(8,128)(2,1)} %all-gather.6.cloned.1.call-done, f32[2048]{0:T(1024)S(1)} %copy-done.3), kind=kOutput, calls=%fused_computation.42 | convolution fusion | flops 17184063488 | bytes 29368320 | tf_op jit(solution)/shard_map/dot_general | solution.py:49
  265.4 0.1 fusion.26
  265.6 0.0 copy-start.1
  265.6 1.3 collective-permute-start.1
  266.9 3.1 collective-permute-start
  269.9 0.0 copy-done
  269.9 0.1 fusion.27
  270.0 0.0 collective-permute-done.1
  270.0 1.9 collective-permute-done
  271.9 0.8 maximum_convert_fusion
  272.7 0.0 copy-done.1
  272.7 27.4 %fusion.17 = bf16[8,2,64,2048]{3,2,1,0:T(8,128)(2,1)} fusion(f32[10,2,64,2048]{3,2,1,0:T(8,128)S(1)} %maximum_convert_fusion, f32[2048]{0:T(1024)S(1)} %bitcast.32, f32[2048]{0:T(1024)S(1)} %bitcast.33, f32[2048]{0:T(1024)S(1)} %bitcast.26, f32[2048]{0:T(1024)S(1)} %bitcast.27, f32[2048]{0:T(1024)S(1)} %bitcast.28, f32[2048]{0:T(1024)S(1)} %bitcast.29, ...), kind=kLoop, calls=%fused_computation.25 | loop fusion | flops 174063616 | bytes 39927808 | tf_op jit(solution)/shard_map/convert_element_type | solution.py:59
  300.2 55.7 %all-gather.8.cloned.1.call-done = bf16[2048,4096]{1,0:T(8,128)(2,1)} async-done(((bf16[2048,1024]{1,0:T(8,128)(2,1)}), bf16[2048,4096]{1,0:T(8,128)(2,1)}) %all-gather.8.cloned.1.call-update) | async-done | bytes 16777232 | tf_op jit(solution)/shard_map/all_gather | solution.py:60
  355.9 23.4 %convolution_bitcast_fusion = f32[4096,1024]{0,1:T(8,128)} fusion(bf16[1024,2048]{1,0:T(8,128)(2,1)} %bitcast.22, bf16[2048,4096]{1,0:T(8,128)(2,1)} %all-gather.8.cloned.1.call-done), kind=kOutput, calls=%fused_computation.7 | convolution fusion | flops 17179869184 | bytes 37748736 | tf_op jit(solution)/shard_map/dot_general | solution.py:62
  379.3 0.0 copy-start.2
  379.3 0.0 reduce-scatter.2.cloned.1.call-update
  379.3 280.3 %reduce-scatter.2.cloned.1.call-done = f32[512,1024]{0,1:T(8,128)} async-done(((f32[4096,1024]{0,1:T(8,128)}), f32[512,1024]{0,1:T(8,128)}) %reduce-scatter.2.cloned.1.call-update) | async-done | bytes 2097168 | tf_op jit(solution)/shard_map/reduce_scatter | solution.py:61
  659.6 0.0 copy-done.2
  659.6 2.8 fusion.25
Async XLA Ops:
  6.5 236.2 %copy-start.3 = (f32[2048]{0:T(1024)S(1)}, f32[2048]{0:T(1024)}, u32[]{:S(2)}) copy-start(f32[2048]{0:T(1024)} %param.9) | copy-start | bytes 24580
  6.5 130.5 %all-gather.4.cloned.1.call-start = ((), (), s32[]{:S(2)}) async-start(), calls=%async_computation.1 | async-start | bytes 9437184 | tf_op jit(solution)/shard_map/all_gather | solution.py:50
  7.3 235.5 %all-gather.6.cloned.1.call-start = ((), (), s32[]{:S(2)}) async-start(), calls=%async_computation.2 | async-start | bytes 20971520 | tf_op jit(solution)/shard_map/all_gather | solution.py:48
  8.0 347.9 %all-gather.8.cloned.1.call-start = ((), (), s32[]{:S(2)}) async-start(), calls=%async_computation.3 | async-start | bytes 20971520 | tf_op jit(solution)/shard_map/all_gather | solution.py:60
  8.7 261.2 %copy-start = (f32[9,2048]{1,0:T(8,128)S(1)}, f32[9,2048]{1,0:T(8,128)}, u32[]{:S(2)}) copy-start(f32[9,2048]{1,0:T(8,128)} %param.10) | copy-start | bytes 221188
  8.8 650.8 %reduce-scatter.2.cloned.1.call-start = ((), (), s32[]{:S(2)}) async-start(), calls=%async_computation.4 | async-start | bytes 18874368 | tf_op jit(solution)/shard_map/reduce_scatter | solution.py:61
  265.6 7.2 %copy-start.1 = (f32[2048]{0:T(1024)S(1)}, f32[2048]{0:T(1024)}, u32[]{:S(2)}) copy-start(f32[2048]{0:T(1024)} %param.11) | copy-start | bytes 24580
  265.6 4.4 collective-permute-start.1
  266.9 5.0 collective-permute-start
  379.3 280.3 %copy-start.2 = (f32[512]{0:T(512)S(1)}, f32[512]{0:T(512)}, u32[]{:S(2)}) copy-start(f32[512]{0:T(512)} %param.13) | copy-start | bytes 6148
Sparse Core Ops, SparseCore 0:
  9.4 127.6 all-gather.3
  138.6 104.0 all-gather.5
  244.3 111.5 all-gather.7
  379.4 280.1 reduce-scatter.1
where the time goes:
time: 669 us
  waiting for transfers between devices  574 us (86%)
  matrix products  46.1 us (7%)
  other arithmetic  31.1 us (5%)
  between operations  13.2 us (2%)
    reduce_scatter x1, waiting for transfers between devices, local(): lax.psum_scatter(lax.dot_general(w_cols, act, (((0,), (1,)), ((), ())), p...  280 us
    all_gather x1, waiting for transfers between devices, local(): lax.all_gather(tokens, 'ch', axis=1, tiled=True)  128 us
    all_gather x1, waiting for transfers between devices, local(): w_whole = lax.all_gather(w_in, 'tok', axis=0, tiled=True)  106 us
    all_gather x1, waiting for transfers between devices, local(): w_cols = lax.all_gather(w_out, 'tok', axis=1, tiled=True)  55.7 us
    convert_element_type x1, other arithmetic, local(): jax.nn.gelu(conv, approximate=False).astype(jnp.bfloat16)  27.4 us
    dot_general x1, matrix products, local(): lax.dot_general(w_cols, act, (((0,), (1,)), ((), ())), preferred_element_...  23.4 us
    dot_general x1, matrix products, local(): jnp.dot(lax.all_gather(tokens, 'ch', axis=1, tiled=True), w_whole, prefer...  22.7 us
  transfers between devices with their start and end apart: 6, of which 5 were waited for; matrix products, arithmetic and copies ran while one was open for 8% of the time, Pallas kernels for 0%

commit v1 on v0

--- a/solution.py
+++ b/solution.py
@@ -57,7 +57,20 @@
     padded = pad_columns(fetch_rims(grid).astype(jnp.float32))
     conv = conv_taps(padded, dw_kernel, dw_bias, height, GRIDW)
     act = jax.nn.gelu(conv, approximate=False).astype(jnp.bfloat16).reshape(rows, hidden)
-    w_cols = lax.all_gather(w_out, "tok", axis=1, tiled=True)
+
+    def notes_serve(matrix):
+        k_all = lax.axis_size("tok")
+        history = [matrix]
+        for d in range(k_all - 1):
+            k_now = lax.ppermute(
+                history[-1], "tok", [(idx, (idx + 1) % k_all) for idx in range(k_all)]
+            )
+            history.append(k_now)
+        taken_in = jnp.concatenate(history[::-1], axis=1)
+        odd = lax.axis_index("tok")
+        return jnp.roll(taken_in, (odd + 1) * matrix.shape[1], axis=1)
+
+    w_cols = notes_serve(w_out)
     flipped = lax.psum_scatter(
         lax.dot_general(w_cols, act, (((0,), (1,)), ((), ())), preferred_element_type=jnp.float32),
         "ch",

time: 669 us -> 627 us (0.937)
  waiting for transfers between devices: 574 us -> 498 us
  local copies, waits for them, and re-layouts: 0.17 us -> 33 us
    ppermute x0 -> x3, waiting for transfers between devices: none -> 152 us  [notes_serve(): lax.ppermute(history[-1], 'tok', [(idx, (idx + 1) % k_all) for idx in ran...]
    all_gather x1, waiting for transfers between devices: 128 us -> 0.01 us  [local(): lax.all_gather(tokens, 'ch', axis=1, tiled=True)]
    all_gather x1 -> x0, waiting for transfers between devices: 55.7 us -> none  [local(): w_cols = lax.all_gather(w_out, 'tok', axis=1, tiled=True)]
    all_gather x1, waiting for transfers between devices: 106 us -> 59.8 us  [local(): w_whole = lax.all_gather(w_in, 'tok', axis=0, tiled=True)]
    unnamed x8 -> x23, local copies, waits for them, and re-layouts: 0.02 us -> 27.9 us
  transfers between devices with their start and end apart: 6 -> 8, of which waited for: 5 -> 5; matrix products, arithmetic and copies ran while one was open for 8% -> 5% of each run, Pallas kernels for 0% -> 0%
where the time goes in v1:
time: 627 us
  waiting for transfers between devices  498 us (79%)
  matrix products  46.4 us (7%)
  local copies, waits for them, and re-layouts  33 us (5%)
  other arithmetic  30 us (5%)
  between operations  13.2 us (2%)
    reduce_scatter x1, waiting for transfers between devices, local(): lax.psum_scatter(lax.dot_general(w_cols, act, (((0,), (1,)), ((), ())), p...  285 us
    ppermute x3, waiting for transfers between devices, notes_serve(): lax.ppermute(history[-1], 'tok', [(idx, (idx + 1) % k_all) for idx in ran...  152 us
    all_gather x1, waiting for transfers between devices, local(): w_whole = lax.all_gather(w_in, 'tok', axis=0, tiled=True)  59.8 us
    unnamed x23, local copies, waits for them, and re-layouts  27.9 us
    convert_element_type x1, other arithmetic, local(): jax.nn.gelu(conv, approximate=False).astype(jnp.bfloat16)  27.4 us
    dot_general x1, matrix products, local(): lax.dot_general(w_cols, act, (((0,), (1,)), ((), ())), preferred_element_...  23.6 us
    dot_general x1, matrix products, local(): jnp.dot(lax.all_gather(tokens, 'ch', axis=1, tiled=True), w_whole, prefer...  22.8 us
  transfers between devices with their start and end apart: 8, of which 5 were waited for; matrix products, arithmetic and copies ran while one was open for 5% of the time, Pallas kernels for 0%

profile of v1, /device:TPU:0, one launch (start us, length us, event | category | flops | bytes accessed | tf_op | source)
XLA Modules:
  0.0 626.6 jit_solution(5711182243731829285)
XLA Ops:
  6.5 0.7 all-gather.3.cloned.1.call-update
  7.3 0.0 all-gather.5.cloned.1.call-start
  7.3 0.7 all-gather.5.cloned.1.call-update
  8.0 0.0 reduce-scatter.2.cloned.1.call-start
  8.1 0.5 collective-permute-start
  8.6 48.3 %collective-permute-done = bf16[2048,1024]{1,0:T(8,128)(2,1)S(1)} collective-permute-done((bf16[2048,1024]{1,0:T(8,128)(2,1)}, bf16[2048,1024]{1,0:T(8,128)(2,1)S(1)}, u32[]{:S(2)}, u32[]{:S(2)}) %collective-permute-start) | collective-permute-done | bytes 4194336 | tf_op jit(solution)/shard_map/ppermute | solution.py:65
  56.9 1.9 copy-done.2
  58.9 0.0 collective-permute-start.1
  58.9 48.0 %collective-permute-done.1 = bf16[2048,1024]{1,0:T(8,128)(2,1)} collective-permute-done((bf16[2048,1024]{1,0:T(8,128)(2,1)S(1)}, bf16[2048,1024]{1,0:T(8,128)(2,1)}, u32[]{:S(2)}, u32[]{:S(2)}) %collective-permute-start.1) | collective-permute-done | bytes 4194336 | tf_op jit(solution)/shard_map/ppermute | solution.py:65
  106.9 1.3 fusion.30
  108.2 55.5 %collective-permute-done.2 = bf16[2048,1024]{1,0:T(8,128)(2,1)} collective-permute-done((bf16[2048,1024]{1,0:T(8,128)(2,1)}, bf16[2048,1024]{1,0:T(8,128)(2,1)}, u32[]{:S(2)}, u32[]{:S(2)}) %collective-permute-start.2) | collective-permute-done | bytes 4194336 | tf_op jit(solution)/shard_map/ppermute | solution.py:65
  163.7 4.6 constant_dynamic-update-slice_fusion.7
  168.3 4.8 constant_dynamic-update-slice_fusion.6
  173.1 2.4 constant_dynamic-update-slice_fusion.5
  175.5 2.5 constant_dynamic-update-slice_fusion.4
  178.0 4.7 constant_dynamic-update-slice_fusion.3
  182.7 4.6 constant_dynamic-update-slice_fusion.2
  187.3 59.8 %all-gather.5.cloned.1.call-done = bf16[4096,2048]{1,0:T(8,128)(2,1)} async-done(((bf16[1024,2048]{1,0:T(8,128)(2,1)}), bf16[4096,2048]{1,0:T(8,128)(2,1)}) %all-gather.5.cloned.1.call-update) | async-done | bytes 16777232 | tf_op jit(solution)/shard_map/all_gather | solution.py:48
  247.1 22.8 %add_convert_fusion = bf16[1024,2048]{1,0:T(8,128)(2,1)S(1)} fusion(bf16[1024,4096]{1,0:T(8,128)(2,1)} %all-gather.3.cloned.1.call-done, bf16[4096,2048]{1,0:T(8,128)(2,1)} %all-gather.5.cloned.1.call-done, f32[2048]{0:T(1024)S(1)} %copy-done.7), kind=kOutput, calls=%fused_computation.43 | convolution fusion | flops 17184063488 | bytes 29368320 | tf_op jit(solution)/shard_map/dot_general | solution.py:49
  269.9 0.0 copy-start.1
  269.9 0.1 fusion.29
  270.0 1.6 collective-permute-start.4
  271.6 3.2 collective-permute-start.3
  274.9 2.4 constant_dynamic-update-slice_fusion.1
  277.3 2.4 constant_dynamic-update-slice_fusion
  279.7 0.8 maximum_convert_fusion
  280.5 27.4 %fusion.19 = bf16[8,2,64,2048]{3,2,1,0:T(8,128)(2,1)} fusion(f32[10,2,64,2048]{3,2,1,0:T(8,128)S(1)} %maximum_convert_fusion, f32[2048]{0:T(1024)S(1)} %bitcast.29, f32[2048]{0:T(1024)S(1)} %bitcast.30, f32[2048]{0:T(1024)S(1)} %bitcast.23, f32[2048]{0:T(1024)S(1)} %bitcast.24, f32[2048]{0:T(1024)S(1)} %bitcast.25, f32[2048]{0:T(1024)S(1)} %bitcast.26, ...), kind=kLoop, calls=%fused_computation.26 | loop fusion | flops 174063616 | bytes 39927808 | tf_op jit(solution)/shard_map/convert_element_type | solution.py:59
  307.9 23.6 %fusion = f32[4096,1024]{1,0:T(8,128)} fusion(bf16[1024,2048]{1,0:T(8,128)(2,1)} %bitcast.19, bf16[2048,8192]{1,0:T(8,128)(2,1)} %constant_dynamic-update-slice_fusion, s32[]{:T(128)S(6)} %select_n.14), kind=kOutput, calls=%fused_computation | convolution fusion | flops 17179869184 | bytes 37748740 | tf_op jit(solution)/shard_map/dot_general | solution.py:75
  331.6 0.0 reduce-scatter.2.cloned.1.call-update
  331.6 285.4 %reduce-scatter.2.cloned.1.call-done = f32[512,1024]{1,0:T(8,128)} async-done(((f32[4096,1024]{1,0:T(8,128)}), f32[512,1024]{1,0:T(8,128)}) %reduce-scatter.2.cloned.1.call-update) | async-done | bytes 2097168 | tf_op jit(solution)/shard_map/reduce_scatter | solution.py:74
  617.0 1.8 fusion.27
  618.8 1.3 copy.8
  (19 shorter events, 0.0 us)
Async XLA Ops:
  6.5 180.8 %all-gather.3.cloned.1.call-start = ((), (), s32[]{:S(2)}) async-start(), calls=%async_computation.1 | async-start | bytes 9437184 | tf_op jit(solution)/shard_map/all_gather | solution.py:50
  7.3 239.8 %all-gather.5.cloned.1.call-start = ((), (), s32[]{:S(2)}) async-start(), calls=%async_computation.2 | async-start | bytes 20971520 | tf_op jit(solution)/shard_map/all_gather | solution.py:48
  8.0 609.0 %reduce-scatter.2.cloned.1.call-start = ((), (), s32[]{:S(2)}) async-start(), calls=%async_computation.3 | async-start | bytes 18874368 | tf_op jit(solution)/shard_map/reduce_scatter | solution.py:74
  8.1 48.9 %collective-permute-start = (bf16[2048,1024]{1,0:T(8,128)(2,1)}, bf16[2048,1024]{1,0:T(8,128)(2,1)S(1)}, u32[]{:S(2)}, u32[]{:S(2)}) collective-permute-start(bf16[2048,1024]{1,0:T(8,128)(2,1)} %param.12), channel_id=1, source_target_pairs={{0,8},{8,16},{16,24},{24,0},{1,9},{9,17},{17,25},{25,1},{2,10},{10... | collective-permute-start | bytes 12582920 | tf_op jit(solution)/shard_map/ppermute | solution.py:65
  56.9 1.9 copy-start.2
  58.9 48.0 %collective-permute-start.1 = (bf16[2048,1024]{1,0:T(8,128)(2,1)S(1)}, bf16[2048,1024]{1,0:T(8,128)(2,1)}, u32[]{:S(2)}, u32[]{:S(2)}) collective-permute-start(bf16[2048,1024]{1,0:T(8,128)(2,1)S(1)} %collective-permute-done), channel_id=1, source_target_pairs={{0,8},{8,16},{16,24},{24,0},{1,9},{9,17},{17,25},{25,1},{2,10},{10... | collective-permute-start | bytes 12582920 | tf_op jit(solution)/shard_map/ppermute | solution.py:65
  106.9 56.8 %collective-permute-start.2 = (bf16[2048,1024]{1,0:T(8,128)(2,1)}, bf16[2048,1024]{1,0:T(8,128)(2,1)}, u32[]{:S(2)}, u32[]{:S(2)}) collective-permute-start(bf16[2048,1024]{1,0:T(8,128)(2,1)} %collective-permute-done.1), channel_id=1, source_target_pairs={{0,8},{8,16},{16,24},{24,0},{1,9},{9,17},{17,25},{25,1},{2,10},{10... | collective-permute-start | bytes 12582920 | tf_op jit(solution)/shard_map/ppermute | solution.py:65
  108.2 64.8 %copy-start.3 = (bf16[2048,1024]{1,0:T(8,128)(2,1)S(1)}, bf16[2048,1024]{1,0:T(8,128)(2,1)}, u32[]{:S(2)}) copy-start(bf16[2048,1024]{1,0:T(8,128)(2,1)} %copy-done.2) | copy-start | bytes 12582916
  168.3 7.2 %copy-start = (bf16[2048,1024]{1,0:T(8,128)(2,1)S(1)}, bf16[2048,1024]{1,0:T(8,128)(2,1)}, u32[]{:S(2)}) copy-start(bf16[2048,1024]{1,0:T(8,128)(2,1)} %param.12) | copy-start | bytes 12582916
  178.0 69.1 %copy-start.7 = (f32[2048]{0:T(1024)S(1)}, f32[2048]{0:T(1024)}, u32[]{:S(2)}) copy-start(f32[2048]{0:T(1024)} %param.9) | copy-start | bytes 24580
  247.1 27.8 %copy-start.4 = (bf16[2048,1024]{1,0:T(8,128)(2,1)S(1)}, bf16[2048,1024]{1,0:T(8,128)(2,1)}, u32[]{:S(2)}) copy-start(bf16[2048,1024]{1,0:T(8,128)(2,1)} %copy-done.2) | copy-start | bytes 12582916
  269.9 7.4 %copy-start.1 = (bf16[2048,1024]{1,0:T(8,128)(2,1)S(1)}, bf16[2048,1024]{1,0:T(8,128)(2,1)}, u32[]{:S(2)}) copy-start(bf16[2048,1024]{1,0:T(8,128)(2,1)} %param.12) | copy-start | bytes 12582916
  270.0 9.6 %collective-permute-start.4 = (bf16[1,2,64,2048]{3,2,1,0:T(8,128)(2,1)S(1)}, bf16[1,2,64,2048]{3,2,1,0:T(8,128)(2,1)S(1)}, u32[]{:S(2)}, u32[]{:S(2)}) collective-permute-start(bf16[1,2,64,2048]{3,2,1,0:T(8,128)(2,1)S(1)} %bitcast.21), channel_id=1, source_target_pairs={{8,0},{16,8},{24,16},{9,1},{17,9},{25,17},{10,2},{18,10},{26,18},{... | collective-permute-start | bytes 1572872 | tf_op jit(solution)/shard_map/ppermute | solution.py:18
  271.6 8.1 %collective-permute-start.3 = (bf16[1,2,64,2048]{3,2,1,0:T(8,128)(2,1)S(1)}, bf16[1,2,64,2048]{3,2,1,0:T(8,128)(2,1)S(1)}, u32[]{:S(2)}, u32[]{:S(2)}) collective-permute-start(bf16[1,2,64,2048]{3,2,1,0:T(8,128)(2,1)S(1)} %bitcast.20), channel_id=1, source_target_pairs={{0,8},{8,16},{16,24},{1,9},{9,17},{17,25},{2,10},{10,18},{18,26},{... | collective-permute-start | bytes 1572872 | tf_op jit(solution)/shard_map/ppermute | solution.py:17
  279.6 0.9 copy-start.5
  331.6 285.4 %copy-start.6 = (f32[512]{0:T(512)S(1)}, f32[512]{0:T(512)}, u32[]{:S(2)}) copy-start(f32[512]{0:T(512)} %param.13) | copy-start | bytes 6148
Sparse Core Ops, SparseCore 0:
  9.4 127.6 all-gather.2
  138.6 108.4 all-gather.4
  331.7 285.2 reduce-scatter.1
